TPU v7x, 32 devices: a whole 2x2x4 slice. The times are simulated.
32 devices in a mesh: dp: 8 (over z, core), seq: 4 (over y, x).
Axes of the slice: x: 2, y: 2, z: 4, core: 2. Of those that a mesh axis runs over, the one named last changes fastest.
Arguments:
- enc_final: bfloat16 [8, 96, 4096], P('dp', 'seq'), may hold values from -6 to 6
- norm_gain: float32 [4096], replicated, may hold values from 0.1 to 1.9
- dec_queries: bfloat16 [2, 8, 512, 2048], P(None, 'dp', 'seq'), may hold values from -48 to 48
- out_grad: bfloat16 [2, 8, 512, 2048], P(None, 'dp', 'seq'), may hold values from -6 to 6
- enc_keys: bfloat16 [2, 8, 96, 2048], P(None, 'dp', 'seq'), may hold values from -6 to 6
- enc_values: bfloat16 [2, 8, 96, 2048], P(None, 'dp', 'seq'), may hold values from -6 to 6
- key_weight: bfloat16 [2, 4096, 2048], P(None, None, 'seq'), may hold values from -0.09375 to 0.09375
- value_weight: bfloat16 [2, 4096, 2048], P(None, None, 'seq'), may hold values from -0.09375 to 0.09375
Outputs:
- enc_grad: bfloat16 [8, 96, 4096], P('dp', 'seq')
- gain_grad: float32 [4096], replicated
All inputs are finite; a program needn't handle non-finite values.
Results may differ from a plain program's by a relative error of at most 0.007.
Values may be sent and summed in bfloat16 or wider, within the bound.
No kernel may reach another device: no remote copies, remote signals or barrier semaphores. Data moves between devices by JAX's collectives and lax.ppermute only.
A program may use at most 128 MiB of HBM per device.

v0:
```python
import jax
import jax.numpy as jnp
from jax import lax
from jax.sharding import PartitionSpec as P

HEAD_DIM = 64


def head_grads(query_rows, grad_rows, key_rows, value_rows, head_size):
    dec_count = query_rows.shape[0]
    enc_count = key_rows.shape[0]
    head_count = query_rows.shape[1] // head_size
    query_heads = query_rows.reshape(dec_count, head_count, head_size)
    grad_heads = grad_rows.reshape(dec_count, head_count, head_size)
    key_heads = key_rows.reshape(enc_count, head_count, head_size)
    value_heads = value_rows.reshape(enc_count, head_count, head_size)
    scores = jnp.einsum("qhd,khd->hqk", query_heads, key_heads, preferred_element_type=jnp.float32)
    row_peak = jnp.max(scores, axis=-1, keepdims=True)
    shifted = jnp.exp(scores - row_peak)
    weights = shifted / jnp.sum(shifted, axis=-1, keepdims=True)
    prob_grad = jnp.einsum(
        "qhd,khd->hqk", grad_heads, value_heads, preferred_element_type=jnp.float32
    )
    row_delta = jnp.sum(weights * prob_grad, axis=-1, keepdims=True)
    score_grad = (weights * (prob_grad - row_delta)).astype(jnp.bfloat16)
    value_grad = jnp.einsum(
        "hqk,qhd->khd", weights.astype(jnp.bfloat16), grad_heads, preferred_element_type=jnp.float32
    )
    key_grad = jnp.einsum(
        "hqk,qhd->khd", score_grad, query_heads, preferred_element_type=jnp.float32
    )
    return (key_grad.reshape(enc_count, -1), value_grad.reshape(enc_count, -1))


def body(
    enc_final, norm_gain, dec_queries, out_grad, enc_keys, enc_values, key_weight, value_weight
):
    layer_count = dec_queries.shape[0]
    head_size = HEAD_DIM
    key_parts = []
    value_parts = []
    for layer_index in range(layer_count):
        query_rows = dec_queries[layer_index, 0]
        grad_rows = out_grad[layer_index, 0]
        key_rows = enc_keys[layer_index, 0]
        value_rows = enc_values[layer_index, 0]
        query_cols, grad_cols, key_cols, value_cols = (
            lax.all_to_all(query_rows, "seq", split_axis=1, concat_axis=0, tiled=True),
            lax.all_to_all(grad_rows, "seq", split_axis=1, concat_axis=0, tiled=True),
            lax.all_to_all(key_rows, "seq", split_axis=1, concat_axis=0, tiled=True),
            lax.all_to_all(value_rows, "seq", split_axis=1, concat_axis=0, tiled=True),
        )
        key_sum, value_sum = head_grads(query_cols, grad_cols, key_cols, value_cols, head_size)
        key_parts.append(key_sum.astype(jnp.bfloat16))
        value_parts.append(value_sum.astype(jnp.bfloat16))
    model_width = enc_final.shape[2]
    running = jnp.zeros((lax.axis_size("seq") * enc_final.shape[1], model_width), jnp.float32)
    for layer_index in range(layer_count):
        key_slice = key_parts[layer_index]
        value_slice = value_parts[layer_index]
        running = running + jnp.einsum(
            "rc,dc->rd", key_slice, key_weight[layer_index], preferred_element_type=jnp.float32
        )
        running = running + jnp.einsum(
            "rc,dc->rd", value_slice, value_weight[layer_index], preferred_element_type=jnp.float32
        )
    state_grad = lax.psum_scatter(running, "seq", scatter_dimension=0, tiled=True)
    final_float = enc_final[0].astype(jnp.float32)
    inv_rms = lax.rsqrt(jnp.mean(final_float * final_float, axis=-1, keepdims=True) + 1e-06)
    normed = final_float * inv_rms
    scaled = norm_gain[None, :] * state_grad
    grad_rows_out = inv_rms * (scaled - normed * jnp.mean(scaled * normed, axis=-1, keepdims=True))
    gain_term = jnp.sum(state_grad * normed, axis=0)
    gain_piece = lax.psum_scatter(gain_term, "seq", scatter_dimension=0, tiled=True)
    gain_piece = lax.psum(gain_piece, "dp")
    gain_total = lax.all_gather(gain_piece, "seq", axis=0, tiled=True)
    gain_grad = gain_total / lax.axis_size("dp")
    return (grad_rows_out.astype(jnp.bfloat16)[None], gain_grad)


def solution(mesh):
    placed = (
        P("dp", "seq", None),
        P(),
        P(None, "dp", "seq", None),
        P(None, "dp", "seq", None),
        P(None, "dp", "seq", None),
        P(None, "dp", "seq", None),
        P(None, None, "seq"),
        P(None, None, "seq"),
    )
    return jax.shard_map(
        body, mesh=mesh, in_specs=placed, out_specs=(P("dp", "seq", None), P()), check_vma=False
    )
```

profile of v0, /device:TPU:0, one launch (start us, length us, event | category | flops | bytes accessed | tf_op | source)
XLA Modules:
  0.0 180.6 jit_solution(3794831154180647183)
XLA Ops:
  8.9 5.2 %all-to-all-start.1 = ((bf16[24,4,512]{2,0,1:T(8,128)(2,1)}), bf16[24,4,512]{2,0,1:T(8,128)(2,1)S(1)}, u32[]{:S(2)}, u32[]{:S(2)}) async-start(bf16[24,4,512]{2,0,1:T(8,128)(2,1)} %copy.32), calls=%async_computation.1 | async-start | bytes 196608 | tf_op jit(solution)/shard_map/all_to_all | solution.py:50
  15.8 3.3 %all-to-all-done.1 = bf16[24,4,512]{2,0,1:T(8,128)(2,1)S(1)} async-done(((bf16[24,4,512]{2,0,1:T(8,128)(2,1)}), bf16[24,4,512]{2,0,1:T(8,128)(2,1)S(1)}, u32[]{:S(2)}, u32[]{:S(2)}) %all-to-all-start.1) | async-done | bytes 98336 | tf_op jit(solution)/shard_map/all_to_all | solution.py:50
  19.1 3.3 %all-to-all-start.3 = ((bf16[24,4,512]{2,0,1:T(8,128)(2,1)}), bf16[24,4,512]{2,0,1:T(8,128)(2,1)S(1)}, u32[]{:S(2)}, u32[]{:S(2)}) async-start(bf16[24,4,512]{2,0,1:T(8,128)(2,1)} %copy.36), calls=%async_computation.3 | async-start | bytes 196608 | tf_op jit(solution)/shard_map/all_to_all | solution.py:51
  23.1 4.2 %all-to-all-done.3 = bf16[24,4,512]{2,0,1:T(8,128)(2,1)S(1)} async-done(((bf16[24,4,512]{2,0,1:T(8,128)(2,1)}), bf16[24,4,512]{2,0,1:T(8,128)(2,1)S(1)}, u32[]{:S(2)}, u32[]{:S(2)}) %all-to-all-start.3) | async-done | bytes 98336 | tf_op jit(solution)/shard_map/all_to_all | solution.py:51
  27.3 3.3 %all-to-all-start.5 = ((bf16[24,4,512]{2,0,1:T(8,128)(2,1)}), bf16[24,4,512]{2,0,1:T(8,128)(2,1)S(1)}, u32[]{:S(2)}, u32[]{:S(2)}) async-start(bf16[24,4,512]{2,0,1:T(8,128)(2,1)} %copy.40), calls=%async_computation.5 | async-start | bytes 196608 | tf_op jit(solution)/shard_map/all_to_all | solution.py:50
  31.3 4.2 %all-to-all-done.5 = bf16[24,4,512]{2,0,1:T(8,128)(2,1)S(1)} async-done(((bf16[24,4,512]{2,0,1:T(8,128)(2,1)}), bf16[24,4,512]{2,0,1:T(8,128)(2,1)S(1)}, u32[]{:S(2)}, u32[]{:S(2)}) %all-to-all-start.5) | async-done | bytes 98336 | tf_op jit(solution)/shard_map/all_to_all | solution.py:50
  35.5 3.3 %all-to-all-start.7 = ((bf16[24,4,512]{2,0,1:T(8,128)(2,1)}), bf16[24,4,512]{2,0,1:T(8,128)(2,1)S(1)}, u32[]{:S(2)}, u32[]{:S(2)}) async-start(bf16[24,4,512]{2,0,1:T(8,128)(2,1)} %copy.44), calls=%async_computation.7 | async-start | bytes 196608 | tf_op jit(solution)/shard_map/all_to_all | solution.py:51
  39.9 3.8 %all-to-all-done.7 = bf16[24,4,512]{2,0,1:T(8,128)(2,1)S(1)} async-done(((bf16[24,4,512]{2,0,1:T(8,128)(2,1)}), bf16[24,4,512]{2,0,1:T(8,128)(2,1)S(1)}, u32[]{:S(2)}, u32[]{:S(2)}) %all-to-all-start.7) | async-done | bytes 98336 | tf_op jit(solution)/shard_map/all_to_all | solution.py:51
  43.7 3.5 %all-to-all-start = ((bf16[128,4,512]{0,2,1:T(8,128)(2,1)}), bf16[128,4,512]{0,2,1:T(8,128)(2,1)S(1)}, u32[]{:S(2)}, u32[]{:S(2)}) async-start(bf16[128,4,512]{0,2,1:T(8,128)(2,1)} %bitcast.1), calls=%async_computation | async-start | bytes 1048576 | tf_op jit(solution)/shard_map/all_to_all | solution.py:48
  48.3 5.4 %all-to-all-done = bf16[128,4,512]{0,2,1:T(8,128)(2,1)S(1)} async-done(((bf16[128,4,512]{0,2,1:T(8,128)(2,1)}), bf16[128,4,512]{0,2,1:T(8,128)(2,1)S(1)}, u32[]{:S(2)}, u32[]{:S(2)}) %all-to-all-start) | async-done | bytes 524320 | tf_op jit(solution)/shard_map/all_to_all | solution.py:48
  53.7 3.5 %all-to-all-start.2 = ((bf16[128,4,512]{0,2,1:T(8,128)(2,1)}), bf16[128,4,512]{0,2,1:T(8,128)(2,1)S(1)}, u32[]{:S(2)}, u32[]{:S(2)}) async-start(bf16[128,4,512]{0,2,1:T(8,128)(2,1)} %bitcast.4), calls=%async_computation.2 | async-start | bytes 1048576 | tf_op jit(solution)/shard_map/all_to_all | solution.py:49
  58.2 6.5 %all-to-all-done.2 = bf16[128,4,512]{0,2,1:T(8,128)(2,1)S(1)} async-done(((bf16[128,4,512]{0,2,1:T(8,128)(2,1)}), bf16[128,4,512]{0,2,1:T(8,128)(2,1)S(1)}, u32[]{:S(2)}, u32[]{:S(2)}) %all-to-all-start.2) | async-done | bytes 524320 | tf_op jit(solution)/shard_map/all_to_all | solution.py:49
  64.8 3.5 %all-to-all-start.4 = ((bf16[128,4,512]{0,2,1:T(8,128)(2,1)}), bf16[128,4,512]{0,2,1:T(8,128)(2,1)S(1)}, u32[]{:S(2)}, u32[]{:S(2)}) async-start(bf16[128,4,512]{0,2,1:T(8,128)(2,1)} %bitcast.13), calls=%async_computation.4 | async-start | bytes 1048576 | tf_op jit(solution)/shard_map/all_to_all | solution.py:48
  73.9 3.1 %all-to-all-done.4 = bf16[128,4,512]{0,2,1:T(8,128)(2,1)S(1)} async-done(((bf16[128,4,512]{0,2,1:T(8,128)(2,1)}), bf16[128,4,512]{0,2,1:T(8,128)(2,1)S(1)}, u32[]{:S(2)}, u32[]{:S(2)}) %all-to-all-start.4) | async-done | bytes 524320 | tf_op jit(solution)/shard_map/all_to_all | solution.py:48
  77.0 3.5 %all-to-all-start.6 = ((bf16[128,4,512]{0,2,1:T(8,128)(2,1)}), bf16[128,4,512]{0,2,1:T(8,128)(2,1)S(1)}, u32[]{:S(2)}, u32[]{:S(2)}) async-start(bf16[128,4,512]{0,2,1:T(8,128)(2,1)} %bitcast.16), calls=%async_computation.6 | async-start | bytes 1048576 | tf_op jit(solution)/shard_map/all_to_all | solution.py:49
  80.7 2.1 %convolution_convert_fusion.2 = bf16[8,96,64]{1,2,0:T(8,128)(2,1)} fusion(bf16[512,8,64]{0,2,1:T(8,128)(2,1)} %reshape.99, f32[8,512,96]{1,2,0:T(8,128)S(1)} %get-tuple-element.13, f32[8,512]{1,0:T(8,128)S(1)} %get-tuple-element.12), kind=kOutput, calls=%fused_computation.24 | convolution fusion | flops 51167232 | bytes 2211840 | tf_op jit(solution)/shard_map/hqk,qhd->khd/dot_general | solution.py:26
  83.9 2.9 %multiply_reduce_fusion.1 = (f32[8,512]{1,0:T(8,128)S(1)}, f32[8,512,96]{1,2,0:T(8,128)}) fusion(f32[8,512,96]{1,2,0:T(8,128)} %copy-done.1, f32[8,512]{1,0:T(8,128)S(1)} %get-tuple-element.12, bf16[512,8,64]{0,2,1:T(8,128)(2,1)S(1)} %copy-done.5, bf16[96,8,64]{2,1,0:T(8,128)(2,1)S(1)} %copy-done.11), kind=kOutput, calls=%fused_computation.19 | convolution fusion | flops 51507200 | bytes 3801088 | tf_op jit(solution)/shard_map/qhd,khd->hqk/dot_general | solution.py:21
  95.3 1.4 convolution_add_fusion.2
  98.1 2.6 %convolution_add_fusion = f32[96,4096]{1,0:T(8,128)} fusion(f32[96,4096]{1,0:T(8,128)S(1)} %convolution_add_fusion.1, bf16[96,512]{0,1:T(8,128)(2,1)S(1)} %bitcast.86, bf16[2,4096,512]{2,1,0:T(8,128)(2,1)S(1)} %bitcast.74), kind=kOutput, calls=%fused_computation.2 | convolution fusion | flops 403046400 | bytes 7471104 | tf_op jit(solution)/shard_map/rc,dc->rd/dot_general | solution.py:64
  102.7 30.5 %reduce-scatter.4.cloned.1.call-done = f32[24,4096]{1,0:T(8,128)} async-done(((f32[96,4096]{1,0:T(8,128)}), f32[24,4096]{1,0:T(8,128)}) %reduce-scatter.4.cloned.1.call-update) | async-done | bytes 393232
  134.5 15.1 %all-reduce.1 = f32[4096]{0:T(1024)S(1)} all-reduce(f32[4096]{0:T(1024)S(1)} %get-tuple-element.2), channel_id=3, replica_groups=mesh['dp'=8,'seq'=4] {'seq'}, use_global_device_ids=true, to_apply=%region_10.0.clone | all-reduce | flops 4096 | bytes 32768
  149.6 13.6 %psum.7 = f32[1024]{0:T(1024)S(1)} all-reduce(f32[1024]{0:T(1024)S(1)} %dynamic-slice.3), channel_id=1, replica_groups=mesh['dp'=8,'seq'=4] {'dp'}, use_global_device_ids=true, to_apply=%region_11.0 | all-reduce | flops 1024 | bytes 8192 | tf_op jit(solution)/shard_map/psum | solution.py:75
  163.3 8.1 %all_gather.3 = f32[4096]{0:T(1024)S(1)} all-gather(f32[1024]{0:T(1024)S(1)} %psum.7), channel_id=1, replica_groups=mesh['dp'=8,'seq'=4] {'seq'}, dimensions={0}, use_global_device_ids=true | all-gather | bytes 20480 | tf_op jit(solution)/shard_map/all_gather | solution.py:76
  172.0 1.8 %fusion.28 = bf16[1,24,4096]{2,1,0:T(8,128)(2,1)} fusion(f32[24,4096]{1,0:T(8,128)} %reduce-scatter.4.cloned.1.call-done, bf16[1,24,4096]{2,1,0:T(8,128)(2,1)S(1)} %copy-done, f32[24]{0:T(128)S(1)} %broadcast_multiply_fusion.1, f32[4096]{0:T(1024)S(1)} %copy-done.13, f32[24]{0:T(128)S(1)} %add_rsqrt_fusion), kind=kLoop, calls=%fused_computation.43 | loop fusion | flops 688128 | bytes 803008 | tf_op jit(solution)/shard_map/broadcast_in_dim | solution.py:78
  (88 shorter events, 28.1 us)
Async XLA Ops:
  7.2 31.6 %copy-start.3 = (bf16[2,1,128,2048]{3,2,1,0:T(8,128)(2,1)S(1)}, bf16[2,1,128,2048]{3,2,1,0:T(8,128)(2,1)}, u32[]{:S(2)}) copy-start(bf16[2,1,128,2048]{3,2,1,0:T(8,128)(2,1)} %param.10) | copy-start | bytes 3145732
  8.9 10.1 %all-to-all-start.1 = ((bf16[24,4,512]{2,0,1:T(8,128)(2,1)}), bf16[24,4,512]{2,0,1:T(8,128)(2,1)S(1)}, u32[]{:S(2)}, u32[]{:S(2)}) async-start(bf16[24,4,512]{2,0,1:T(8,128)(2,1)} %copy.32), calls=%async_computation.1 | async-start | bytes 196608 | tf_op jit(solution)/shard_map/all_to_all | solution.py:50
  19.1 8.2 %all-to-all-start.3 = ((bf16[24,4,512]{2,0,1:T(8,128)(2,1)}), bf16[24,4,512]{2,0,1:T(8,128)(2,1)S(1)}, u32[]{:S(2)}, u32[]{:S(2)}) async-start(bf16[24,4,512]{2,0,1:T(8,128)(2,1)} %copy.36), calls=%async_computation.3 | async-start | bytes 196608 | tf_op jit(solution)/shard_map/all_to_all | solution.py:51
  27.3 8.2 %all-to-all-start.5 = ((bf16[24,4,512]{2,0,1:T(8,128)(2,1)}), bf16[24,4,512]{2,0,1:T(8,128)(2,1)S(1)}, u32[]{:S(2)}, u32[]{:S(2)}) async-start(bf16[24,4,512]{2,0,1:T(8,128)(2,1)} %copy.40), calls=%async_computation.5 | async-start | bytes 196608 | tf_op jit(solution)/shard_map/all_to_all | solution.py:50
  35.5 3.3 %copy-start.6 = (bf16[24,4,512]{2,0,1:T(8,128)(2,1)}, bf16[24,4,512]{2,0,1:T(8,128)(2,1)S(1)}, u32[]{:S(2)}) copy-start(bf16[24,4,512]{2,0,1:T(8,128)(2,1)S(1)} %all-to-all-done.5) | copy-start | bytes 294916
  35.5 8.2 %all-to-all-start.7 = ((bf16[24,4,512]{2,0,1:T(8,128)(2,1)}), bf16[24,4,512]{2,0,1:T(8,128)(2,1)S(1)}, u32[]{:S(2)}, u32[]{:S(2)}) async-start(bf16[24,4,512]{2,0,1:T(8,128)(2,1)} %copy.44), calls=%async_computation.7 | async-start | bytes 196608 | tf_op jit(solution)/shard_map/all_to_all | solution.py:51
  38.9 8.3 %copy-start.4 = (bf16[2,1,128,2048]{3,2,1,0:T(8,128)(2,1)S(1)}, bf16[2,1,128,2048]{3,2,1,0:T(8,128)(2,1)}, u32[]{:S(2)}) copy-start(bf16[2,1,128,2048]{3,2,1,0:T(8,128)(2,1)} %param.11) | copy-start | bytes 3145732
  43.7 3.6 %copy-start.8 = (bf16[24,4,512]{2,0,1:T(8,128)(2,1)}, bf16[24,4,512]{2,0,1:T(8,128)(2,1)S(1)}, u32[]{:S(2)}) copy-start(bf16[24,4,512]{2,0,1:T(8,128)(2,1)S(1)} %all-to-all-done.7) | copy-start | bytes 294916
  43.7 10.0 %all-to-all-start = ((bf16[128,4,512]{0,2,1:T(8,128)(2,1)}), bf16[128,4,512]{0,2,1:T(8,128)(2,1)S(1)}, u32[]{:S(2)}, u32[]{:S(2)}) async-start(bf16[128,4,512]{0,2,1:T(8,128)(2,1)} %bitcast.1), calls=%async_computation | async-start | bytes 1048576 | tf_op jit(solution)/shard_map/all_to_all | solution.py:48
  53.7 11.0 %all-to-all-start.2 = ((bf16[128,4,512]{0,2,1:T(8,128)(2,1)}), bf16[128,4,512]{0,2,1:T(8,128)(2,1)S(1)}, u32[]{:S(2)}, u32[]{:S(2)}) async-start(bf16[128,4,512]{0,2,1:T(8,128)(2,1)} %bitcast.4), calls=%async_computation.2 | async-start | bytes 1048576 | tf_op jit(solution)/shard_map/all_to_all | solution.py:49
  58.2 12.0 %copy-start.7 = (bf16[24,4,512]{2,0,1:T(8,128)(2,1)S(1)}, bf16[24,4,512]{2,0,1:T(8,128)(2,1)}, u32[]{:S(2)}) copy-start(bf16[24,4,512]{2,0,1:T(8,128)(2,1)} %copy-done.6) | copy-start | bytes 294916
  58.2 12.2 %copy-start.9 = (bf16[24,4,512]{2,0,1:T(8,128)(2,1)S(1)}, bf16[24,4,512]{2,0,1:T(8,128)(2,1)}, u32[]{:S(2)}) copy-start(bf16[24,4,512]{2,0,1:T(8,128)(2,1)} %copy-done.8) | copy-start | bytes 294916
  64.8 12.2 %all-to-all-start.4 = ((bf16[128,4,512]{0,2,1:T(8,128)(2,1)}), bf16[128,4,512]{0,2,1:T(8,128)(2,1)S(1)}, u32[]{:S(2)}, u32[]{:S(2)}) async-start(bf16[128,4,512]{0,2,1:T(8,128)(2,1)} %bitcast.13), calls=%async_computation.4 | async-start | bytes 1048576 | tf_op jit(solution)/shard_map/all_to_all | solution.py:48
  73.9 8.9 %copy-start.1 = (f32[8,512,96]{1,2,0:T(8,128)}, f32[8,512,96]{1,2,0:T(8,128)S(1)}, u32[]{:S(2)}) copy-start(f32[8,512,96]{1,2,0:T(8,128)S(1)} %get-tuple-element.13) | copy-start | bytes 4718596
  77.0 10.0 %all-to-all-start.6 = ((bf16[128,4,512]{0,2,1:T(8,128)(2,1)}), bf16[128,4,512]{0,2,1:T(8,128)(2,1)S(1)}, u32[]{:S(2)}, u32[]{:S(2)}) async-start(bf16[128,4,512]{0,2,1:T(8,128)(2,1)} %bitcast.16), calls=%async_computation.6 | async-start | bytes 1048576 | tf_op jit(solution)/shard_map/all_to_all | solution.py:49
  80.4 52.8 %reduce-scatter.4.cloned.1.call-start = ((), (), s32[]{:S(2)}) async-start(), calls=%async_computation.9 | async-start | bytes 1966080
  88.2 1.5 copy-start.15
  88.2 3.2 %slice-start.2 = ((s8[8388608]{0:T(1024)(128)(4,1)}), s8[4194304]{0:T(1024)(128)(4,1)S(1)}, s32[]{:S(2)}) async-start(s8[8388608]{0:T(1024)(128)(4,1)} %bitcast.75), calls=%async_computation.12 | async-start | bytes 8388608
  89.1 1.9 %copy-start.2 = (f32[8,512,96]{1,2,0:T(8,128)S(1)}, f32[8,512,96]{1,2,0:T(8,128)}, u32[]{:S(2)}) copy-start(f32[8,512,96]{1,2,0:T(8,128)} %copy-done.1) | copy-start | bytes 4718596
  89.1 3.6 %slice-start.3 = ((s8[8388608]{0:T(1024)(128)(4,1)}), s8[4194304]{0:T(1024)(128)(4,1)S(1)}, s32[]{:S(2)}) async-start(s8[8388608]{0:T(1024)(128)(4,1)} %bitcast.75), calls=%async_computation.13 | async-start | bytes 8388608
  91.0 3.6 %slice-start = ((s8[8388608]{0:T(1024)(128)(4,1)}), s8[4194304]{0:T(1024)(128)(4,1)S(1)}, s32[]{:S(2)}) async-start(s8[8388608]{0:T(1024)(128)(4,1)} %bitcast.73), calls=%async_computation.10 | async-start | bytes 8388608
  92.7 2.5 %slice-start.1 = ((s8[8388608]{0:T(1024)(128)(4,1)}), s8[4194304]{0:T(1024)(128)(4,1)S(1)}, s32[]{:S(2)}) async-start(s8[8388608]{0:T(1024)(128)(4,1)} %bitcast.73), calls=%async_computation.11 | async-start | bytes 8388608
  100.7 1.9 %copy-start = (bf16[1,24,4096]{2,1,0:T(8,128)(2,1)S(1)}, bf16[1,24,4096]{2,1,0:T(8,128)(2,1)}, u32[]{:S(2)}) copy-start(bf16[1,24,4096]{2,1,0:T(8,128)(2,1)} %param.8) | copy-start | bytes 589828
  100.7 32.6 %copy-start.13 = (f32[4096]{0:T(1024)S(1)}, f32[4096]{0:T(1024)}, u32[]{:S(2)}) copy-start(f32[4096]{0:T(1024)} %param.9) | copy-start | bytes 49156
  (5 other events, 4.8 us)
Sparse Core Ops, SparseCore 0:
  100.8 32.3 reduce-scatter.3
where the time goes:
time: 182 us; the launch traced here: 181 us
  waiting for transfers between devices  61.1 us (34%)
  blocking collectives  36.8 us (20%)
  starting transfers between devices  29.2 us (16%)
  local copies, waits for them, and re-layouts  20 us (11%)
  between operations  15 us (8%)
  matrix products  14.6 us (8%)
  other arithmetic  3.87 us (2%)
    unnamed x2, waiting for transfers between devices  30.5 us
    unnamed x1, blocking collectives  15.1 us
    psum x1, blocking collectives, body(): gain_piece = lax.psum(gain_piece, 'dp')  13.6 us
    all_to_all x2, waiting for transfers between devices, body(): lax.all_to_all(query_rows, 'seq', split_axis=1, concat_axis=0, tiled=True)  8.5 us
    all_to_all x2, starting transfers between devices, body(): lax.all_to_all(key_rows, 'seq', split_axis=1, concat_axis=0, tiled=True)  8.5 us
    all_gather x1, blocking collectives, body(): gain_total = lax.all_gather(gain_piece, 'seq', axis=0, tiled=True)  8.08 us
    all_to_all x2, waiting for transfers between devices, body(): lax.all_to_all(value_rows, 'seq', split_axis=1, concat_axis=0, tiled=True)  7.94 us
    all_to_all x2, waiting for transfers between devices, body(): lax.all_to_all(key_rows, 'seq', split_axis=1, concat_axis=0, tiled=True)  7.45 us
  transfers between devices with their start and end apart: 9, of which 9 were waited for; matrix products, arithmetic and copies ran while one was open for 10% of the time, Pallas kernels for 0%

commit v1 on v0

--- a/solution.py
+++ b/solution.py
@@ -72,7 +72,11 @@
     grad_rows_out = inv_rms * (scaled - normed * jnp.mean(scaled * normed, axis=-1, keepdims=True))
     gain_term = jnp.sum(state_grad * normed, axis=0)
     gain_piece = lax.psum_scatter(gain_term, "seq", scatter_dimension=0, tiled=True)
-    gain_piece = lax.psum(gain_piece, "dp")
+    gain_piece = gain_piece
+    for hop in (1, 2, 4):
+        gain_piece = gain_piece + lax.ppermute(
+            gain_piece, "dp", [(dev, dev ^ hop) for dev in range(8)]
+        )
     gain_total = lax.all_gather(gain_piece, "seq", axis=0, tiled=True)
     gain_grad = gain_total / lax.axis_size("dp")
     return (grad_rows_out.astype(jnp.bfloat16)[None], gain_grad)

time: 182 us -> 175 us (0.962)
  blocking collectives: 36.8 us -> 23.2 us
  starting transfers between devices: 29.2 us -> 33.1 us
  waiting for transfers between devices: 61.1 us -> 64.8 us
    psum x1 -> x0, blocking collectives: 13.6 us -> none  [body(): gain_piece = lax.psum(gain_piece, 'dp')]
    ppermute x0 -> x3, starting transfers between devices: none -> 3.9 us  [body(): lax.ppermute(gain_piece, 'dp', [(dev, dev ^ hop) for dev in range(8)])]
    ppermute x0 -> x3, waiting for transfers between devices: none -> 3.56 us  [body(): lax.ppermute(gain_piece, 'dp', [(dev, dev ^ hop) for dev in range(8)])]
  transfers between devices with their start and end apart: 9 -> 12, of which waited for: 9 -> 12; matrix products, arithmetic and copies ran while one was open for 10% -> 11% of each run, Pallas kernels for 0% -> 0%
where the time goes in v1:
time: 175 us; the launch traced here: 174 us
  waiting for transfers between devices  64.8 us (37%)
  starting transfers between devices  33.1 us (19%)
  blocking collectives  23.2 us (13%)
  local copies, waits for them, and re-layouts  20 us (11%)
  between operations  15 us (9%)
  matrix products  14.5 us (8%)
  other arithmetic  3.88 us (2%)
    unnamed x2, waiting for transfers between devices  30.5 us
    unnamed x1, blocking collectives  15.1 us
    all_to_all x2, waiting for transfers between devices, body(): lax.all_to_all(query_rows, 'seq', split_axis=1, concat_axis=0, tiled=True)  8.55 us
    all_to_all x2, starting transfers between devices, body(): lax.all_to_all(key_rows, 'seq', split_axis=1, concat_axis=0, tiled=True)  8.5 us
    all_gather x1, blocking collectives, body(): gain_total = lax.all_gather(gain_piece, 'seq', axis=0, tiled=True)  8.07 us
    all_to_all x2, waiting for transfers between devices, body(): lax.all_to_all(value_rows, 'seq', split_axis=1, concat_axis=0, tiled=True)  7.93 us
    all_to_all x2, waiting for transfers between devices, body(): lax.all_to_all(key_rows, 'seq', split_axis=1, concat_axis=0, tiled=True)  7.45 us
    all_to_all x2, starting transfers between devices, body(): lax.all_to_all(query_rows, 'seq', split_axis=1, concat_axis=0, tiled=True)  6.94 us
  transfers between devices with their start and end apart: 12, of which 12 were waited for; matrix products, arithmetic and copies ran while one was open for 11% of the time, Pallas kernels for 0%

profile of v1, /device:TPU:0, one launch (start us, length us, event | category | flops | bytes accessed | tf_op | source)
XLA Modules:
  0.0 174.4 jit_solution(10650280582918020598)
XLA Ops:
  8.9 5.2 %all-to-all-start.1 = ((bf16[24,4,512]{2,0,1:T(8,128)(2,1)}), bf16[24,4,512]{2,0,1:T(8,128)(2,1)S(1)}, u32[]{:S(2)}, u32[]{:S(2)}) async-start(bf16[24,4,512]{2,0,1:T(8,128)(2,1)} %copy.32), calls=%async_computation.1 | async-start | bytes 196608 | tf_op jit(solution)/shard_map/all_to_all | solution.py:50
  15.8 3.3 %all-to-all-done.1 = bf16[24,4,512]{2,0,1:T(8,128)(2,1)S(1)} async-done(((bf16[24,4,512]{2,0,1:T(8,128)(2,1)}), bf16[24,4,512]{2,0,1:T(8,128)(2,1)S(1)}, u32[]{:S(2)}, u32[]{:S(2)}) %all-to-all-start.1) | async-done | bytes 98336 | tf_op jit(solution)/shard_map/all_to_all | solution.py:50
  19.1 3.3 %all-to-all-start.3 = ((bf16[24,4,512]{2,0,1:T(8,128)(2,1)}), bf16[24,4,512]{2,0,1:T(8,128)(2,1)S(1)}, u32[]{:S(2)}, u32[]{:S(2)}) async-start(bf16[24,4,512]{2,0,1:T(8,128)(2,1)} %copy.36), calls=%async_computation.3 | async-start | bytes 196608 | tf_op jit(solution)/shard_map/all_to_all | solution.py:51
  23.1 4.2 %all-to-all-done.3 = bf16[24,4,512]{2,0,1:T(8,128)(2,1)S(1)} async-done(((bf16[24,4,512]{2,0,1:T(8,128)(2,1)}), bf16[24,4,512]{2,0,1:T(8,128)(2,1)S(1)}, u32[]{:S(2)}, u32[]{:S(2)}) %all-to-all-start.3) | async-done | bytes 98336 | tf_op jit(solution)/shard_map/all_to_all | solution.py:51
  27.3 3.3 %all-to-all-start.5 = ((bf16[24,4,512]{2,0,1:T(8,128)(2,1)}), bf16[24,4,512]{2,0,1:T(8,128)(2,1)S(1)}, u32[]{:S(2)}, u32[]{:S(2)}) async-start(bf16[24,4,512]{2,0,1:T(8,128)(2,1)} %copy.40), calls=%async_computation.5 | async-start | bytes 196608 | tf_op jit(solution)/shard_map/all_to_all | solution.py:50
  31.3 4.2 %all-to-all-done.5 = bf16[24,4,512]{2,0,1:T(8,128)(2,1)S(1)} async-done(((bf16[24,4,512]{2,0,1:T(8,128)(2,1)}), bf16[24,4,512]{2,0,1:T(8,128)(2,1)S(1)}, u32[]{:S(2)}, u32[]{:S(2)}) %all-to-all-start.5) | async-done | bytes 98336 | tf_op jit(solution)/shard_map/all_to_all | solution.py:50
  35.5 3.3 %all-to-all-start.7 = ((bf16[24,4,512]{2,0,1:T(8,128)(2,1)}), bf16[24,4,512]{2,0,1:T(8,128)(2,1)S(1)}, u32[]{:S(2)}, u32[]{:S(2)}) async-start(bf16[24,4,512]{2,0,1:T(8,128)(2,1)} %copy.44), calls=%async_computation.7 | async-start | bytes 196608 | tf_op jit(solution)/shard_map/all_to_all | solution.py:51
  40.0 3.7 %all-to-all-done.7 = bf16[24,4,512]{2,0,1:T(8,128)(2,1)S(1)} async-done(((bf16[24,4,512]{2,0,1:T(8,128)(2,1)}), bf16[24,4,512]{2,0,1:T(8,128)(2,1)S(1)}, u32[]{:S(2)}, u32[]{:S(2)}) %all-to-all-start.7) | async-done | bytes 98336 | tf_op jit(solution)/shard_map/all_to_all | solution.py:51
  43.7 3.5 %all-to-all-start = ((bf16[128,4,512]{0,2,1:T(8,128)(2,1)}), bf16[128,4,512]{0,2,1:T(8,128)(2,1)S(1)}, u32[]{:S(2)}, u32[]{:S(2)}) async-start(bf16[128,4,512]{0,2,1:T(8,128)(2,1)} %bitcast.1), calls=%async_computation | async-start | bytes 1048576 | tf_op jit(solution)/shard_map/all_to_all | solution.py:48
  48.3 5.4 %all-to-all-done = bf16[128,4,512]{0,2,1:T(8,128)(2,1)S(1)} async-done(((bf16[128,4,512]{0,2,1:T(8,128)(2,1)}), bf16[128,4,512]{0,2,1:T(8,128)(2,1)S(1)}, u32[]{:S(2)}, u32[]{:S(2)}) %all-to-all-start) | async-done | bytes 524320 | tf_op jit(solution)/shard_map/all_to_all | solution.py:48
  53.7 3.5 %all-to-all-start.2 = ((bf16[128,4,512]{0,2,1:T(8,128)(2,1)}), bf16[128,4,512]{0,2,1:T(8,128)(2,1)S(1)}, u32[]{:S(2)}, u32[]{:S(2)}) async-start(bf16[128,4,512]{0,2,1:T(8,128)(2,1)} %bitcast.4), calls=%async_computation.2 | async-start | bytes 1048576 | tf_op jit(solution)/shard_map/all_to_all | solution.py:49
  58.2 6.5 %all-to-all-done.2 = bf16[128,4,512]{0,2,1:T(8,128)(2,1)S(1)} async-done(((bf16[128,4,512]{0,2,1:T(8,128)(2,1)}), bf16[128,4,512]{0,2,1:T(8,128)(2,1)S(1)}, u32[]{:S(2)}, u32[]{:S(2)}) %all-to-all-start.2) | async-done | bytes 524320 | tf_op jit(solution)/shard_map/all_to_all | solution.py:49
  64.8 3.5 %all-to-all-start.4 = ((bf16[128,4,512]{0,2,1:T(8,128)(2,1)}), bf16[128,4,512]{0,2,1:T(8,128)(2,1)S(1)}, u32[]{:S(2)}, u32[]{:S(2)}) async-start(bf16[128,4,512]{0,2,1:T(8,128)(2,1)} %bitcast.13), calls=%async_computation.4 | async-start | bytes 1048576 | tf_op jit(solution)/shard_map/all_to_all | solution.py:48
  73.8 3.1 %all-to-all-done.4 = bf16[128,4,512]{0,2,1:T(8,128)(2,1)S(1)} async-done(((bf16[128,4,512]{0,2,1:T(8,128)(2,1)}), bf16[128,4,512]{0,2,1:T(8,128)(2,1)S(1)}, u32[]{:S(2)}, u32[]{:S(2)}) %all-to-all-start.4) | async-done | bytes 524320 | tf_op jit(solution)/shard_map/all_to_all | solution.py:48
  77.0 3.5 %all-to-all-start.6 = ((bf16[128,4,512]{0,2,1:T(8,128)(2,1)}), bf16[128,4,512]{0,2,1:T(8,128)(2,1)S(1)}, u32[]{:S(2)}, u32[]{:S(2)}) async-start(bf16[128,4,512]{0,2,1:T(8,128)(2,1)} %bitcast.16), calls=%async_computation.6 | async-start | bytes 1048576 | tf_op jit(solution)/shard_map/all_to_all | solution.py:49
  80.7 2.1 %convolution_convert_fusion.2 = bf16[8,96,64]{1,2,0:T(8,128)(2,1)} fusion(bf16[512,8,64]{0,2,1:T(8,128)(2,1)} %reshape.99, f32[8,512,96]{1,2,0:T(8,128)S(1)} %get-tuple-element.13, f32[8,512]{1,0:T(8,128)S(1)} %get-tuple-element.12), kind=kOutput, calls=%fused_computation.24 | convolution fusion | flops 51167232 | bytes 2211840 | tf_op jit(solution)/shard_map/hqk,qhd->khd/dot_general | solution.py:26
  83.9 2.9 %multiply_reduce_fusion.1 = (f32[8,512]{1,0:T(8,128)S(1)}, f32[8,512,96]{1,2,0:T(8,128)}) fusion(f32[8,512,96]{1,2,0:T(8,128)} %copy-done.1, f32[8,512]{1,0:T(8,128)S(1)} %get-tuple-element.12, bf16[512,8,64]{0,2,1:T(8,128)(2,1)S(1)} %copy-done.5, bf16[96,8,64]{2,1,0:T(8,128)(2,1)S(1)} %copy-done.11), kind=kOutput, calls=%fused_computation.19 | convolution fusion | flops 51507200 | bytes 3801088 | tf_op jit(solution)/shard_map/qhd,khd->hqk/dot_general | solution.py:21
  98.1 2.6 %convolution_add_fusion = f32[96,4096]{1,0:T(8,128)} fusion(f32[96,4096]{1,0:T(8,128)S(1)} %convolution_add_fusion.1, bf16[96,512]{0,1:T(8,128)(2,1)S(1)} %bitcast.86, bf16[2,4096,512]{2,1,0:T(8,128)(2,1)S(1)} %bitcast.74), kind=kOutput, calls=%fused_computation.2 | convolution fusion | flops 403046400 | bytes 7471104 | tf_op jit(solution)/shard_map/rc,dc->rd/dot_general | solution.py:64
  102.7 30.5 %reduce-scatter.4.cloned.1.call-done = f32[24,4096]{1,0:T(8,128)} async-done(((f32[96,4096]{1,0:T(8,128)}), f32[24,4096]{1,0:T(8,128)}) %reduce-scatter.4.cloned.1.call-update) | async-done | bytes 393232
  134.5 15.1 %all-reduce.1 = f32[4096]{0:T(1024)S(1)} all-reduce(f32[4096]{0:T(1024)S(1)} %get-tuple-element.2), channel_id=3, replica_groups=mesh['dp'=8,'seq'=4] {'seq'}, use_global_device_ids=true, to_apply=%region_10.0.clone | all-reduce | flops 4096 | bytes 32768
  152.3 2.1 %collective-permute-done.1 = f32[1024]{0:T(1024)S(1)} collective-permute-done((f32[1024]{0:T(1024)S(1)}, f32[1024]{0:T(1024)S(1)}, u32[]{:S(2)}, u32[]{:S(2)}) %collective-permute-start.1) | collective-permute-done | bytes 4128 | tf_op jit(solution)/shard_map/ppermute | solution.py:77
  154.4 2.4 %collective-permute-start.2 = (f32[1024]{0:T(1024)S(1)}, f32[1024]{0:T(1024)S(1)}, u32[]{:S(2)}, u32[]{:S(2)}) collective-permute-start(f32[1024]{0:T(1024)S(1)} %add.35), channel_id=1, source_target_pairs={{0,16},{4,20},{8,24},{12,28},{16,0},{20,4},{24,8},{28,12},{1,17},{... | collective-permute-start | bytes 12296 | tf_op jit(solution)/shard_map/ppermute | solution.py:77
  156.8 1.8 %fusion.28 = bf16[1,24,4096]{2,1,0:T(8,128)(2,1)} fusion(f32[24,4096]{1,0:T(8,128)} %reduce-scatter.4.cloned.1.call-done, bf16[1,24,4096]{2,1,0:T(8,128)(2,1)S(1)} %copy-done, f32[24]{0:T(128)S(1)} %broadcast_multiply_fusion.1, f32[4096]{0:T(1024)S(1)} %copy-done.13, f32[24]{0:T(128)S(1)} %add_rsqrt_fusion), kind=kLoop, calls=%fused_computation.43 | loop fusion | flops 688128 | bytes 803008 | tf_op jit(solution)/shard_map/broadcast_in_dim | solution.py:82
  158.9 8.1 %all_gather.3 = f32[4096]{0:T(1024)S(1)} all-gather(f32[1024]{0:T(1024)S(1)} %add.36), channel_id=1, replica_groups=mesh['dp'=8,'seq'=4] {'seq'}, dimensions={0}, use_global_device_ids=true | all-gather | bytes 20480 | tf_op jit(solution)/shard_map/all_gather | solution.py:80
  (96 shorter events, 32.4 us)
Async XLA Ops:
  7.2 31.6 %copy-start.3 = (bf16[2,1,128,2048]{3,2,1,0:T(8,128)(2,1)S(1)}, bf16[2,1,128,2048]{3,2,1,0:T(8,128)(2,1)}, u32[]{:S(2)}) copy-start(bf16[2,1,128,2048]{3,2,1,0:T(8,128)(2,1)} %param.10) | copy-start | bytes 3145732
  8.9 10.1 %all-to-all-start.1 = ((bf16[24,4,512]{2,0,1:T(8,128)(2,1)}), bf16[24,4,512]{2,0,1:T(8,128)(2,1)S(1)}, u32[]{:S(2)}, u32[]{:S(2)}) async-start(bf16[24,4,512]{2,0,1:T(8,128)(2,1)} %copy.32), calls=%async_computation.1 | async-start | bytes 196608 | tf_op jit(solution)/shard_map/all_to_all | solution.py:50
  19.1 8.2 %all-to-all-start.3 = ((bf16[24,4,512]{2,0,1:T(8,128)(2,1)}), bf16[24,4,512]{2,0,1:T(8,128)(2,1)S(1)}, u32[]{:S(2)}, u32[]{:S(2)}) async-start(bf16[24,4,512]{2,0,1:T(8,128)(2,1)} %copy.36), calls=%async_computation.3 | async-start | bytes 196608 | tf_op jit(solution)/shard_map/all_to_all | solution.py:51
  27.3 8.2 %all-to-all-start.5 = ((bf16[24,4,512]{2,0,1:T(8,128)(2,1)}), bf16[24,4,512]{2,0,1:T(8,128)(2,1)S(1)}, u32[]{:S(2)}, u32[]{:S(2)}) async-start(bf16[24,4,512]{2,0,1:T(8,128)(2,1)} %copy.40), calls=%async_computation.5 | async-start | bytes 196608 | tf_op jit(solution)/shard_map/all_to_all | solution.py:50
  35.5 3.3 %copy-start.6 = (bf16[24,4,512]{2,0,1:T(8,128)(2,1)}, bf16[24,4,512]{2,0,1:T(8,128)(2,1)S(1)}, u32[]{:S(2)}) copy-start(bf16[24,4,512]{2,0,1:T(8,128)(2,1)S(1)} %all-to-all-done.5) | copy-start | bytes 294916
  35.5 8.2 %all-to-all-start.7 = ((bf16[24,4,512]{2,0,1:T(8,128)(2,1)}), bf16[24,4,512]{2,0,1:T(8,128)(2,1)S(1)}, u32[]{:S(2)}, u32[]{:S(2)}) async-start(bf16[24,4,512]{2,0,1:T(8,128)(2,1)} %copy.44), calls=%async_computation.7 | async-start | bytes 196608 | tf_op jit(solution)/shard_map/all_to_all | solution.py:51
  38.9 8.3 %copy-start.4 = (bf16[2,1,128,2048]{3,2,1,0:T(8,128)(2,1)S(1)}, bf16[2,1,128,2048]{3,2,1,0:T(8,128)(2,1)}, u32[]{:S(2)}) copy-start(bf16[2,1,128,2048]{3,2,1,0:T(8,128)(2,1)} %param.11) | copy-start | bytes 3145732
  43.7 3.6 %copy-start.8 = (bf16[24,4,512]{2,0,1:T(8,128)(2,1)}, bf16[24,4,512]{2,0,1:T(8,128)(2,1)S(1)}, u32[]{:S(2)}) copy-start(bf16[24,4,512]{2,0,1:T(8,128)(2,1)S(1)} %all-to-all-done.7) | copy-start | bytes 294916
  43.7 10.0 %all-to-all-start = ((bf16[128,4,512]{0,2,1:T(8,128)(2,1)}), bf16[128,4,512]{0,2,1:T(8,128)(2,1)S(1)}, u32[]{:S(2)}, u32[]{:S(2)}) async-start(bf16[128,4,512]{0,2,1:T(8,128)(2,1)} %bitcast.1), calls=%async_computation | async-start | bytes 1048576 | tf_op jit(solution)/shard_map/all_to_all | solution.py:48
  53.7 11.0 %all-to-all-start.2 = ((bf16[128,4,512]{0,2,1:T(8,128)(2,1)}), bf16[128,4,512]{0,2,1:T(8,128)(2,1)S(1)}, u32[]{:S(2)}, u32[]{:S(2)}) async-start(bf16[128,4,512]{0,2,1:T(8,128)(2,1)} %bitcast.4), calls=%async_computation.2 | async-start | bytes 1048576 | tf_op jit(solution)/shard_map/all_to_all | solution.py:49
  58.2 12.0 %copy-start.7 = (bf16[24,4,512]{2,0,1:T(8,128)(2,1)S(1)}, bf16[24,4,512]{2,0,1:T(8,128)(2,1)}, u32[]{:S(2)}) copy-start(bf16[24,4,512]{2,0,1:T(8,128)(2,1)} %copy-done.6) | copy-start | bytes 294916
  58.2 12.2 %copy-start.9 = (bf16[24,4,512]{2,0,1:T(8,128)(2,1)S(1)}, bf16[24,4,512]{2,0,1:T(8,128)(2,1)}, u32[]{:S(2)}) copy-start(bf16[24,4,512]{2,0,1:T(8,128)(2,1)} %copy-done.8) | copy-start | bytes 294916
  64.8 12.2 %all-to-all-start.4 = ((bf16[128,4,512]{0,2,1:T(8,128)(2,1)}), bf16[128,4,512]{0,2,1:T(8,128)(2,1)S(1)}, u32[]{:S(2)}, u32[]{:S(2)}) async-start(bf16[128,4,512]{0,2,1:T(8,128)(2,1)} %bitcast.13), calls=%async_computation.4 | async-start | bytes 1048576 | tf_op jit(solution)/shard_map/all_to_all | solution.py:48
  73.8 9.0 %copy-start.1 = (f32[8,512,96]{1,2,0:T(8,128)}, f32[8,512,96]{1,2,0:T(8,128)S(1)}, u32[]{:S(2)}) copy-start(f32[8,512,96]{1,2,0:T(8,128)S(1)} %get-tuple-element.13) | copy-start | bytes 4718596
  77.0 10.0 %all-to-all-start.6 = ((bf16[128,4,512]{0,2,1:T(8,128)(2,1)}), bf16[128,4,512]{0,2,1:T(8,128)(2,1)S(1)}, u32[]{:S(2)}, u32[]{:S(2)}) async-start(bf16[128,4,512]{0,2,1:T(8,128)(2,1)} %bitcast.16), calls=%async_computation.6 | async-start | bytes 1048576 | tf_op jit(solution)/shard_map/all_to_all | solution.py:49
  80.4 52.8 %reduce-scatter.4.cloned.1.call-start = ((), (), s32[]{:S(2)}) async-start(), calls=%async_computation.9 | async-start | bytes 1966080
  88.2 3.2 %slice-start.2 = ((s8[8388608]{0:T(1024)(128)(4,1)}), s8[4194304]{0:T(1024)(128)(4,1)S(1)}, s32[]{:S(2)}) async-start(s8[8388608]{0:T(1024)(128)(4,1)} %bitcast.75), calls=%async_computation.12 | async-start | bytes 8388608
  89.1 3.6 %slice-start.3 = ((s8[8388608]{0:T(1024)(128)(4,1)}), s8[4194304]{0:T(1024)(128)(4,1)S(1)}, s32[]{:S(2)}) async-start(s8[8388608]{0:T(1024)(128)(4,1)} %bitcast.75), calls=%async_computation.13 | async-start | bytes 8388608
  91.0 3.6 %slice-start = ((s8[8388608]{0:T(1024)(128)(4,1)}), s8[4194304]{0:T(1024)(128)(4,1)S(1)}, s32[]{:S(2)}) async-start(s8[8388608]{0:T(1024)(128)(4,1)} %bitcast.73), calls=%async_computation.10 | async-start | bytes 8388608
  92.7 2.5 %slice-start.1 = ((s8[8388608]{0:T(1024)(128)(4,1)}), s8[4194304]{0:T(1024)(128)(4,1)S(1)}, s32[]{:S(2)}) async-start(s8[8388608]{0:T(1024)(128)(4,1)} %bitcast.73), calls=%async_computation.11 | async-start | bytes 8388608
  100.7 32.6 %copy-start.13 = (f32[4096]{0:T(1024)S(1)}, f32[4096]{0:T(1024)}, u32[]{:S(2)}) copy-start(f32[4096]{0:T(1024)} %param.9) | copy-start | bytes 49156
  149.6 1.2 collective-permute-start
  150.8 3.6 %collective-permute-start.1 = (f32[1024]{0:T(1024)S(1)}, f32[1024]{0:T(1024)S(1)}, u32[]{:S(2)}, u32[]{:S(2)}) collective-permute-start(f32[1024]{0:T(1024)S(1)} %dynamic-slice_add_fusion), channel_id=1, source_target_pairs={{0,8},{4,12},{8,0},{12,4},{16,24},{20,28},{24,16},{28,20},{1,9},{5... | collective-permute-start | bytes 12296 | tf_op jit(solution)/shard_map/ppermute | solution.py:77
  154.4 4.5 %collective-permute-start.2 = (f32[1024]{0:T(1024)S(1)}, f32[1024]{0:T(1024)S(1)}, u32[]{:S(2)}, u32[]{:S(2)}) collective-permute-start(f32[1024]{0:T(1024)S(1)} %add.35), channel_id=1, source_target_pairs={{0,16},{4,20},{8,24},{12,28},{16,0},{20,4},{24,8},{28,12},{1,17},{... | collective-permute-start | bytes 12296 | tf_op jit(solution)/shard_map/ppermute | solution.py:77
  (8 other events, 10.1 us)
Sparse Core Ops, SparseCore 0:
  100.8 32.3 reduce-scatter.3
